TPU v7x, 256 devices: a whole 4x4x8 slice. The times are simulated.
256 devices in a mesh: rep: 2 (over core), src: 16 (over z_lo, x), tgt: 8 (over z_hi, y).
Axes of the slice: x: 4, y: 4, z: 8 (z_hi: 2, z_lo: 4; z = z_hi * 4 + z_lo), core: 2. Of those that a mesh axis runs over, the one named last changes fastest.
Arguments:
- src_feats: float32 [2, 2048, 3200], P('rep', ('src', 'tgt')), may hold values from -6 to 6
- tgt_cotangent: float32 [2, 2048, 3200], P('rep', ('tgt', 'src')), may hold values from -0.6 to 0.6
- rotation: float32 [2, 16, 8, 115, 384], P('rep', 'src', 'tgt'), may hold values from -3 to 3
- edge_src: int32 [2, 16, 8, 384], P('rep', 'src', 'tgt'), may hold values from 0 to 127
- edge_tgt: int32 [2, 16, 8, 384], P('rep', 'src', 'tgt'), may hold values from 0 to 255
- edge_count: int32 [2, 16, 8], P('rep', 'src', 'tgt'), may hold values from 192 to 384, as said below
- w_zero: float32 [640, 640], replicated, may hold values from -0.25 to 0.25
- w_one_re: float32 [512, 512], replicated, may hold values from -0.1875 to 0.1875
- w_one_im: float32 [512, 512], replicated, may hold values from -0.1875 to 0.1875
- w_two_re: float32 [384, 384], replicated, may hold values from -0.21875 to 0.21875
- w_two_im: float32 [384, 384], replicated, may hold values from -0.21875 to 0.21875
Outputs:
- grad_feats: float32 [2, 2048, 3200], P('rep', ('src', 'tgt'))
- grad_w_zero: float32 [640, 640], P('src')
- grad_w_one_re: float32 [512, 512], P('src')
- grad_w_one_im: float32 [512, 512], P('src')
- grad_w_two_re: float32 [384, 384], P('src')
- grad_w_two_im: float32 [384, 384], P('src')
Inputs may be any that keep to these rules, and one draw needn't show every extreme that they name: `edge_count`: some tile of each structure is full.
All inputs are finite; a program needn't handle non-finite values.
Results may differ from a plain program's by a relative error of at most 0.0003.
Values sent between devices are 32-bit elements; how exact they have to be, the bound alone decides.
A program may use at most 128 MiB of HBM per device.

v0:
```python
import jax
import jax.numpy as jnp
from jax import lax
from jax.sharding import PartitionSpec as P

OFFSETS = (0, 1, 10, 35, 70)
HIGH = lax.Precision.HIGHEST


def rotations(wig):
    mats = []
    for level in range(5):
        order = min(level, 2)
        rows = 2 * order + 1
        cols = 2 * level + 1
        piece = wig[OFFSETS[level] : OFFSETS[level] + rows * cols]
        mats.append(piece.reshape(rows, cols, piece.shape[-1]))
    return mats


def group(rotated, count):
    zero = jnp.stack([rotated[v][:, min(v, 2)] for v in range(5)], 1)
    plus_one = jnp.stack([rotated[v][:, min(v, 2) + 1] for v in range(1, 5)], 1)
    minus_one = jnp.stack([rotated[v][:, min(v, 2) - 1] for v in range(1, 5)], 1)
    plus_two = jnp.stack([rotated[v][:, 4] for v in range(2, 5)], 1)
    minus_two = jnp.stack([rotated[v][:, 0] for v in range(2, 5)], 1)
    return tuple((a.reshape(count, -1) for a in (zero, plus_one, minus_one, plus_two, minus_two)))


def ungroup(groups, count, chans):
    zero, plus_one, minus_one, plus_two, minus_two = [a.reshape(count, -1, chans) for a in groups]
    result = []
    for level in range(5):
        rows = []
        if level >= 2:
            rows.append(minus_two[:, level - 2])
        if level >= 1:
            rows.append(minus_one[:, level - 1])
        rows.append(zero[:, level])
        if level >= 1:
            rows.append(plus_one[:, level - 1])
        if level >= 2:
            rows.append(plus_two[:, level - 2])
        result.append(jnp.stack(rows, 1))
    return result


def tdot(left, right):
    return lax.dot_general(
        left, right, (((0,), (0,)), ((), ())), precision=HIGH, preferred_element_type=jnp.float32
    )


def ntdot(left, right):
    return lax.dot_general(
        left, right, (((1,), (1,)), ((), ())), precision=HIGH, preferred_element_type=jnp.float32
    )


def block_grads(xrows, grows, wig, weights):
    w_zero, w_one_re, w_one_im, w_two_re, w_two_im = weights
    count, coefs, chans = xrows.shape
    mats = rotations(wig)
    xrot = [
        jnp.einsum("rcb,bcf->brf", mats[v], xrows[:, v * v : (v + 1) * (v + 1)], precision=HIGH)
        for v in range(5)
    ]
    grot = [
        jnp.einsum("rcb,bcf->brf", mats[v], grows[:, v * v : (v + 1) * (v + 1)], precision=HIGH)
        for v in range(5)
    ]
    z0, zp1, zm1, zp2, zm2 = group(xrot, count)
    u0, up1, um1, up2, um2 = group(grot, count)
    grads = (
        tdot(z0, u0),
        tdot(zp1, up1) + tdot(zm1, um1),
        tdot(zp1, um1) - tdot(zm1, up1),
        tdot(zp2, up2) + tdot(zm2, um2),
        tdot(zp2, um2) - tdot(zm2, up2),
    )
    d0 = ntdot(u0, w_zero)
    dp1 = ntdot(up1, w_one_re) + ntdot(um1, w_one_im)
    dm1 = ntdot(um1, w_one_re) - ntdot(up1, w_one_im)
    dp2 = ntdot(up2, w_two_re) + ntdot(um2, w_two_im)
    dm2 = ntdot(um2, w_two_re) - ntdot(up2, w_two_im)
    back = ungroup((d0, dp1, dm1, dp2, dm2), count, chans)
    pieces = [jnp.einsum("rcb,brf->bcf", mats[v], back[v], precision=HIGH) for v in range(5)]
    return (jnp.concatenate(pieces, 1), grads)


def local(
    src_feats,
    tgt_cotangent,
    rotation,
    edge_src,
    edge_tgt,
    edge_count,
    w_zero,
    w_one_re,
    w_one_im,
    w_two_re,
    w_two_im,
):
    weights = (w_zero, w_one_re, w_one_im, w_two_re, w_two_im)
    chans = w_zero.shape[0] // 5
    feat = src_feats.shape[2]
    source_block = lax.all_gather(src_feats, "tgt", axis=1, tiled=True)[0]
    target_block = lax.all_gather(tgt_cotangent, "src", axis=1, tiled=True)[0]
    src_blk = source_block.shape[0]
    source_block = source_block.reshape(src_blk, 25, chans)
    target_block = target_block.reshape(target_block.shape[0], 25, chans)
    sources = edge_src[0, 0, 0]
    targets = edge_tgt[0, 0, 0]
    wig = rotation[0, 0, 0]
    live_count = edge_count[0, 0, 0]
    cap = sources.shape[0]
    width = 128
    atom_ids = jnp.arange(src_blk, dtype=jnp.int32)

    def step(index, carry):
        total, sums = carry
        start = index * width
        src_ids = lax.dynamic_slice_in_dim(sources, start, width)
        tgt_ids = lax.dynamic_slice_in_dim(targets, start, width)
        wig_block = lax.dynamic_slice_in_dim(wig, start, width, 1)
        live = (start + jnp.arange(width, dtype=jnp.int32) < live_count).astype(jnp.float32)
        xrows = jnp.take(source_block, src_ids, axis=0) * live[:, None, None]
        grows = jnp.take(target_block, tgt_ids, axis=0) * live[:, None, None]
        term, parts = block_grads(xrows, grows, wig_block, weights)
        onehot = (src_ids[:, None] == atom_ids[None, :]).astype(jnp.float32)
        added = tdot(onehot, term.reshape(width, feat))
        return (total + added, tuple((a + b for a, b in zip(sums, parts))))

    stop = cap // width
    init = (
        jnp.zeros((src_blk, feat), jnp.float32),
        tuple((jnp.zeros(w.shape, jnp.float32) for w in weights)),
    )
    total, sums = lax.fori_loop(0, stop, step, init)
    grad_feats = lax.psum_scatter(total[None], "tgt", scatter_dimension=1, tiled=True)
    summed = lax.psum((sums[0], sums[1], sums[2], sums[3], sums[4]), ("rep", "src", "tgt"))
    owner = lax.axis_index("src")
    parts_count = lax.axis_size("src")
    final = tuple(
        (
            lax.dynamic_slice_in_dim(
                a, owner * (a.shape[0] // parts_count), a.shape[0] // parts_count, 0
            )
            for a in summed
        )
    )
    return (grad_feats, final[0], final[1], final[2], final[3], final[4])


def solution(mesh):
    placed = (
        P("rep", ("src", "tgt"), None),
        P("rep", ("tgt", "src"), None),
        P("rep", "src", "tgt", None, None),
        P("rep", "src", "tgt", None),
        P("rep", "src", "tgt", None),
        P("rep", "src", "tgt"),
        P(),
        P(),
        P(),
        P(),
        P(),
    )
    return jax.shard_map(
        local,
        mesh=mesh,
        in_specs=placed,
        out_specs=(
            P("rep", ("src", "tgt"), None),
            P("src", None),
            P("src", None),
            P("src", None),
            P("src", None),
            P("src", None),
        ),
        check_vma=False,
    )
```

profile of v0, /device:TPU:2, one launch (start us, length us, event | category | flops | bytes accessed | tf_op | source)
XLA Modules:
  0.0 847.1 jit_solution(5621229995447299344)
XLA Ops:
  13.4 70.2 %all-gather.5.cloned.1.call-done = f32[1,128,3200]{2,0,1:T(1,128)} async-done(((f32[1,16,3200]{2,0,1:T(1,128)}), f32[1,128,3200]{2,0,1:T(1,128)}) %all-gather.5.cloned.1.call-update) | async-done | bytes 1638416 | tf_op jit(solution)/shard_map/all_gather | solution.py:107
  83.6 3.4 copy.147
  89.2 79.0 %all-gather.3.cloned.1.call-done = f32[1,256,3200]{2,0,1:T(1,128)} async-done(((f32[1,16,3200]{2,0,1:T(1,128)}), f32[1,256,3200]{2,0,1:T(1,128)}) %all-gather.3.cloned.1.call-update) | async-done | bytes 3276816 | tf_op jit(solution)/shard_map/all_gather | solution.py:108
  168.2 6.0 copy.145
  174.2 3.7 copy.148
  177.9 296.7 %while.24 = (s32[]{:T(128)}, f32[128,3200]{1,0:T(8,128)}, f32[640,640]{1,0:T(8,128)}, f32[512,512]{1,0:T(8,128)}, f32[512,512]{1,0:T(8,128)}, /*index=5*/f32[384...) while((s32[]{:T(128)}, f32[128,3200]{1,0:T(8,128)}, ...), condition=%wide.region_1.0_spmd.clone, body=%wide.region_0.1_spmd.clone.sunk | while | flops 6995169280 | bytes 155906560 | solution.py:139
  193.9 2.9 gather_fusion
  239.1 3.7 fusion.286
  262.8 5.7 concatenate.9
  270.3 3.8 convolution_add_fusion.10
  290.5 2.9 gather_fusion
  320.1 3.3 fusion.304
  329.2 4.1 select_add_fusion.2
  338.2 3.7 fusion.286
  362.1 5.7 concatenate.9
  369.6 4.3 convolution_add_fusion.10
  390.1 2.9 gather_fusion
  419.8 3.3 fusion.304
  428.9 4.1 select_add_fusion.2
  438.0 3.7 fusion.286
  461.6 5.7 concatenate.9
  469.1 4.3 convolution_add_fusion.10
  475.2 271.2 %all-reduce.3.cloned.1.call-done = (f32[640,640]{1,0:T(8,128)}, f32[512,512]{1,0:T(8,128)}, f32[512,512]{1,0:T(8,128)}, f32[384,384]{1,0:T(8,128)}, f32[384,384]{1,0:T(8,128)}) async-done(((f32[640,640]{1,0:T(8,128)}, f32[512,512]{1,0:T(8,128)}, f32[512,512]{1,0:T(8,128)}, f32[384,384]{1,0:T(8,128)}, f32[384,384]{1,0:T(8,128)}), (f32[640,640]{1,0:T(8,128)}, f32[512,512]{1,0:T(8,128)}, f32[512,512]{1,0:T(8,128)}, ...) | async-done | bytes 4915216 | tf_op jit(solution)/shard_map/psum | solution.py:141
  750.9 89.4 %reduce-scatter.2.cloned.1.call-done = f32[1,16,3200]{2,1,0:T(8,128)} async-done(((f32[1,128,3200]{2,1,0:T(8,128)}), f32[1,16,3200]{2,1,0:T(8,128)}) %reduce-scatter.2.cloned.1.call-update) | async-done | bytes 204816 | tf_op jit(solution)/shard_map/reduce_scatter | solution.py:140
  (673 shorter events, 240.9 us)
Async XLA Ops:
  7.2 76.4 %all-gather.5.cloned.1.call-start = ((), (), s32[]{:S(2)}) async-start(), calls=%async_computation.2 | async-start | bytes 1843200 | tf_op jit(solution)/shard_map/all_gather | solution.py:107
  9.1 159.1 %all-gather.3.cloned.1.call-start = ((), (), s32[]{:S(2)}) async-start(), calls=%async_computation.1 | async-start | bytes 3481600 | tf_op jit(solution)/shard_map/all_gather | solution.py:108
  11.0 735.5 %all-reduce.3.cloned.1.call-start = ((), (), s32[]{:S(2)}) async-start(), calls=%async_computation.4 | async-start | bytes 9830400 | tf_op jit(solution)/shard_map/psum | solution.py:141
  177.9 5.5 copy-start.48
  177.9 15.9 %copy-start.52 = (s32[384]{0:T(512)}, s32[384]{0:T(512)S(1)}, u32[]{:S(2)}) copy-start(s32[384]{0:T(512)S(1)} %get-tuple-element.817) | copy-start | bytes 4612 | tf_op jit(solution)/shard_map/while
  217.7 4.2 copy-start.38
  217.7 4.2 copy-start.40
  217.7 4.2 copy-start.41
  274.5 5.5 copy-start.48
  274.5 15.9 %copy-start.52 = (s32[384]{0:T(512)}, s32[384]{0:T(512)S(1)}, u32[]{:S(2)}) copy-start(s32[384]{0:T(512)S(1)} %get-tuple-element.817) | copy-start | bytes 4612 | tf_op jit(solution)/shard_map/while
  314.1 4.2 copy-start.38
  314.1 4.2 copy-start.40
  314.1 4.2 copy-start.41
  369.6 4.3 copy-start.49
  369.6 4.3 copy-start.51
  369.6 4.3 copy-start.53
  374.1 5.5 copy-start.48
  374.1 15.9 %copy-start.52 = (s32[384]{0:T(512)}, s32[384]{0:T(512)S(1)}, u32[]{:S(2)}) copy-start(s32[384]{0:T(512)S(1)} %get-tuple-element.817) | copy-start | bytes 4612 | tf_op jit(solution)/shard_map/while
  413.7 4.2 copy-start.38
  413.7 4.2 copy-start.40
  469.1 4.3 copy-start.49
  469.1 4.3 copy-start.51
  469.1 4.3 copy-start.53
  474.6 365.7 %reduce-scatter.2.cloned.1.call-start = ((), (), s32[]{:S(2)}) async-start(), calls=%async_computation.3 | async-start | bytes 1843200 | tf_op jit(solution)/shard_map/reduce_scatter | solution.py:140
  (151 other events, 352.7 us)
Sparse Core Ops, SparseCore 0:
  10.6 72.9 all-gather.4
  86.0 82.1 all-gather.2
  474.7 271.6 all-reduce.2
  750.9 89.3 reduce-scatter.1
where the time goes:
time: 852 us; the launch traced here: 847 us
  waiting for transfers between devices  510 us (60%)
  local copies, waits for them, and re-layouts  145 us (17%)
  matrix products  144 us (17%)
  other arithmetic  28.3 us (3%)
  between operations  14.1 us (2%)
    psum x1, waiting for transfers between devices, local(): lax.psum((sums[0], sums[1], sums[2], sums[3], sums[4]), ('rep', 'src', 't...  271 us
    reduce_scatter x1, waiting for transfers between devices, local(): lax.psum_scatter(total[None], 'tgt', scatter_dimension=1, tiled=True)  89.4 us
    all_gather x1, waiting for transfers between devices, local(): target_block = lax.all_gather(tgt_cotangent, 'src', axis=1, tiled=True)[0]  79 us
    all_gather x1, waiting for transfers between devices, local(): source_block = lax.all_gather(src_feats, 'tgt', axis=1, tiled=True)[0]  70.2 us
    dot_general x30, matrix products, tdot(): lax.dot_general(left, right, (((0,), (0,)), ((), ())), precision=HIGH, pr...  58.3 us
    dot_general x27, matrix products, ntdot(): lax.dot_general(left, right, (((1,), (1,)), ((), ())), precision=HIGH, pr...  39.2 us
    while x357, local copies, waits for them, and re-layouts  25.1 us
    concatenate x6, local copies, waits for them, and re-layouts, block_grads(): return (jnp.concatenate(pieces, 1), grads)  22.6 us
  transfers between devices with their start and end apart: 4, of which 4 were waited for; matrix products, arithmetic and copies ran while one was open for 2% of the time, Pallas kernels for 0%

commit v1 on v0

--- a/solution.py
+++ b/solution.py
@@ -138,7 +138,9 @@
     )
     total, sums = lax.fori_loop(0, stop, step, init)
     grad_feats = lax.psum_scatter(total[None], "tgt", scatter_dimension=1, tiled=True)
-    summed = lax.psum((sums[0], sums[1], sums[2], sums[3], sums[4]), ("rep", "src", "tgt"))
+    summed = lax.psum(
+        lax.psum((sums[0], sums[1], sums[2], sums[3], sums[4]), "rep"), ("src", "tgt")
+    )
     owner = lax.axis_index("src")
     parts_count = lax.axis_size("src")
     final = tuple(

time: 852 us -> 866 us (1.016)
  waiting for transfers between devices: 510 us -> 524 us
    psum x1 -> x2, waiting for transfers between devices: 271 us -> 285 us  [the longest x1 246 us: local(): lax.psum(lax.psum((sums[0], sums[1], sums[2], sums[3], sums[4]), 'rep'),...]
  transfers between devices with their start and end apart: 4 -> 5, of which waited for: 4 -> 5; matrix products, arithmetic and copies ran while one was open for 2% -> 2% of each run, Pallas kernels for 0% -> 0%
where the time goes in v1:
time: 866 us; the launch traced here: 861 us
  waiting for transfers between devices  524 us (61%)
  local copies, waits for them, and re-layouts  145 us (17%)
  matrix products  144 us (17%)
  other arithmetic  28.3 us (3%)
  between operations  14.1 us (2%)
    psum x1, waiting for transfers between devices, local(): lax.psum(lax.psum((sums[0], sums[1], sums[2], sums[3], sums[4]), 'rep'),...  246 us
    reduce_scatter x1, waiting for transfers between devices, local(): lax.psum_scatter(total[None], 'tgt', scatter_dimension=1, tiled=True)  89.5 us
    all_gather x1, waiting for transfers between devices, local(): target_block = lax.all_gather(tgt_cotangent, 'src', axis=1, tiled=True)[0]  79 us
    all_gather x1, waiting for transfers between devices, local(): source_block = lax.all_gather(src_feats, 'tgt', axis=1, tiled=True)[0]  70.2 us
    dot_general x30, matrix products, tdot(): lax.dot_general(left, right, (((0,), (0,)), ((), ())), precision=HIGH, pr...  58.3 us
    psum x1, waiting for transfers between devices, local(): lax.psum((sums[0], sums[1], sums[2], sums[3], sums[4]), 'rep')  39.4 us
    dot_general x27, matrix products, ntdot(): lax.dot_general(left, right, (((1,), (1,)), ((), ())), precision=HIGH, pr...  39.2 us
    while x357, local copies, waits for them, and re-layouts  25.1 us
  transfers between devices with their start and end apart: 5, of which 5 were waited for; matrix products, arithmetic and copies ran while one was open for 2% of the time, Pallas kernels for 0%

profile of v1, /device:TPU:2, one launch (start us, length us, event | category | flops | bytes accessed | tf_op | source)
XLA Modules:
  0.0 861.2 jit_solution(5275825503685481522)
XLA Ops:
  13.4 70.2 %all-gather.5.cloned.1.call-done = f32[1,128,3200]{2,0,1:T(1,128)} async-done(((f32[1,16,3200]{2,0,1:T(1,128)}), f32[1,128,3200]{2,0,1:T(1,128)}) %all-gather.5.cloned.1.call-update) | async-done | bytes 1638416 | tf_op jit(solution)/shard_map/all_gather | solution.py:107
  83.6 3.4 copy.147
  89.2 79.0 %all-gather.3.cloned.1.call-done = f32[1,256,3200]{2,0,1:T(1,128)} async-done(((f32[1,16,3200]{2,0,1:T(1,128)}), f32[1,256,3200]{2,0,1:T(1,128)}) %all-gather.3.cloned.1.call-update) | async-done | bytes 3276816 | tf_op jit(solution)/shard_map/all_gather | solution.py:108
  168.2 6.0 copy.145
  174.2 3.7 copy.148
  177.9 296.6 %while.24 = (s32[]{:T(128)}, f32[128,3200]{1,0:T(8,128)}, f32[640,640]{1,0:T(8,128)}, f32[512,512]{1,0:T(8,128)}, f32[512,512]{1,0:T(8,128)}, /*index=5*/f32[384...) while((s32[]{:T(128)}, f32[128,3200]{1,0:T(8,128)}, ...), condition=%wide.region_1.0_spmd.clone, body=%wide.region_0.1_spmd.clone.sunk | while | flops 6995169280 | bytes 155906560 | solution.py:139
  193.9 2.9 gather_fusion
  239.1 3.7 fusion.286
  262.7 5.7 concatenate.9
  270.3 3.8 convolution_add_fusion.10
  320.1 3.3 fusion.304
  329.1 4.1 select_add_fusion.2
  338.2 3.7 fusion.286
  362.0 5.7 concatenate.9
  369.5 4.3 convolution_add_fusion.10
  390.0 2.9 gather_fusion
  419.7 3.3 fusion.304
  428.8 4.1 select_add_fusion.2
  437.9 3.7 fusion.286
  461.4 5.7 concatenate.9
  469.0 4.3 convolution_add_fusion.10
  474.6 39.4 %all-reduce.7.cloned.1.call-done = (f32[640,640]{1,0:T(8,128)}, f32[512,512]{1,0:T(8,128)}, f32[512,512]{1,0:T(8,128)}, f32[384,384]{1,0:T(8,128)}, f32[384,384]{1,0:T(8,128)}) async-done(((f32[640,640]{1,0:T(8,128)}, f32[512,512]{1,0:T(8,128)}, f32[512,512]{1,0:T(8,128)}, f32[384,384]{1,0:T(8,128)}, f32[384,384]{1,0:T(8,128)}), (f32[640,640]{1,0:T(8,128)}, f32[512,512]{1,0:T(8,128)}, f32[512,512]{1,0:T(8,128)}, ...) | async-done | bytes 4915216 | tf_op jit(solution)/shard_map/psum | solution.py:142
  514.6 245.8 %all-reduce.5.cloned.1.call-done = (f32[640,640]{1,0:T(8,128)}, f32[512,512]{1,0:T(8,128)}, f32[512,512]{1,0:T(8,128)}, f32[384,384]{1,0:T(8,128)}, f32[384,384]{1,0:T(8,128)}) async-done(((f32[640,640]{1,0:T(8,128)}, f32[512,512]{1,0:T(8,128)}, f32[512,512]{1,0:T(8,128)}, f32[384,384]{1,0:T(8,128)}, f32[384,384]{1,0:T(8,128)}), (f32[640,640]{1,0:T(8,128)}, f32[512,512]{1,0:T(8,128)}, f32[512,512]{1,0:T(8,128)}, ...) | async-done | bytes 4915216 | tf_op jit(solution)/shard_map/psum | solution.py:141
  764.9 89.5 %reduce-scatter.2.cloned.1.call-done = f32[1,16,3200]{2,1,0:T(8,128)} async-done(((f32[1,128,3200]{2,1,0:T(8,128)}), f32[1,16,3200]{2,1,0:T(8,128)}) %reduce-scatter.2.cloned.1.call-update) | async-done | bytes 204816 | tf_op jit(solution)/shard_map/reduce_scatter | solution.py:140
  (676 shorter events, 243.7 us)
Async XLA Ops:
  7.2 76.4 %all-gather.5.cloned.1.call-start = ((), (), s32[]{:S(2)}) async-start(), calls=%async_computation.2 | async-start | bytes 1843200 | tf_op jit(solution)/shard_map/all_gather | solution.py:107
  9.1 159.1 %all-gather.3.cloned.1.call-start = ((), (), s32[]{:S(2)}) async-start(), calls=%async_computation.1 | async-start | bytes 3481600 | tf_op jit(solution)/shard_map/all_gather | solution.py:108
  10.9 503.0 %all-reduce.7.cloned.1.call-start = ((), (), s32[]{:S(2)}) async-start(), calls=%async_computation.5 | async-start | bytes 9830400 | tf_op jit(solution)/shard_map/psum | solution.py:142
  177.9 5.5 copy-start.48
  177.9 15.9 %copy-start.52 = (s32[384]{0:T(512)}, s32[384]{0:T(512)S(1)}, u32[]{:S(2)}) copy-start(s32[384]{0:T(512)S(1)} %get-tuple-element.822) | copy-start | bytes 4612 | tf_op jit(solution)/shard_map/while
  217.7 4.2 copy-start.38
  217.7 4.2 copy-start.40
  274.5 5.5 copy-start.48
  274.5 15.9 %copy-start.52 = (s32[384]{0:T(512)}, s32[384]{0:T(512)S(1)}, u32[]{:S(2)}) copy-start(s32[384]{0:T(512)S(1)} %get-tuple-element.822) | copy-start | bytes 4612 | tf_op jit(solution)/shard_map/while
  314.0 4.2 copy-start.38
  314.1 4.2 copy-start.40
  369.5 4.3 copy-start.49
  369.5 4.3 copy-start.51
  369.5 4.3 copy-start.53
  374.0 5.5 copy-start.48
  374.0 15.9 %copy-start.52 = (s32[384]{0:T(512)}, s32[384]{0:T(512)S(1)}, u32[]{:S(2)}) copy-start(s32[384]{0:T(512)S(1)} %get-tuple-element.822) | copy-start | bytes 4612 | tf_op jit(solution)/shard_map/while
  413.6 4.2 copy-start.38
  413.6 4.2 copy-start.40
  413.6 4.2 copy-start.41
  469.0 4.3 copy-start.49
  469.0 4.3 copy-start.51
  469.0 4.3 copy-start.53
  474.5 285.9 %all-reduce.5.cloned.1.call-start = ((), (), s32[]{:S(2)}) async-start(), calls=%async_computation.4 | async-start | bytes 9830400 | tf_op jit(solution)/shard_map/psum | solution.py:141
  514.0 340.4 %reduce-scatter.2.cloned.1.call-start = ((), (), s32[]{:S(2)}) async-start(), calls=%async_computation.3 | async-start | bytes 1843200 | tf_op jit(solution)/shard_map/reduce_scatter | solution.py:140
  (152 other events, 356.6 us)
Sparse Core Ops, SparseCore 0:
  10.6 72.9 all-gather.4
  86.0 82.1 all-gather.2
  474.6 39.3 all-reduce.6
  520.2 240.1 all-reduce.4
  765.5 88.8 reduce-scatter.1
